TPU v7x, 32 devices: a whole 2x2x4 slice. The times are simulated.
32 devices in a mesh: tm: 4 (over z), det: 8 (over y, x, core).
Axes of the slice: x: 2, y: 2, z: 4, core: 2. Of those that a mesh axis runs over, the one named last changes fastest.
Arguments:
- time_stream: bfloat16 [1024, 32768], P('det', 'tm'), may hold values from -6 to 6
- filter_taps: bfloat16 [1024, 129], P('det'), may hold values from -0.5 to 0.5
- det_precision: bfloat16 [1024, 1024], replicated
- left_weight: float32 [128, 32], replicated, may hold values from -0.046875 to 0.046875
- right_weight: float32 [128, 32], replicated, may hold values from -1 to 1
- frame_tile: int32 [32768, 1], P(('tm', 'det')), may hold values from 0 to 63; in each aligned block of 1024 rows (0 to 1023, 1024 to 2047, ...) at most 24 rows name the same one
- tile_owner: int32 [64], replicated, may hold values from 0 to 31, as said below
- frame_count: int32 [32], P(('tm', 'det')), may hold values from 512 to 1024, as said below
Outputs:
- sky_map: float32 [64, 16384], P(('tm', 'det'))
Inputs may be any that keep to these rules, and one draw needn't show every extreme that they name: `frame_tile`: within the frames of one segment (aligned blocks of 1024 rows) no tile is named more than 24 times, a bound that some block reaches. `tile_owner`: every device number is the owner of exactly 2 tiles. `frame_count`: some segment has all 1024 frames live.
All inputs are finite; a program needn't handle non-finite values.
Results may differ from a plain program's by a relative error of at most 0.0041.
Values may be sent and summed in bfloat16 or wider, within the bound.
A program may use at most 64 MiB of HBM per device.

v0:
```python
import jax
import jax.numpy as jnp
from jax import lax
from jax.sharding import PartitionSpec as P

HW = 64
TILE_DEV = 2


def with_halo(block, sides, width):
    for axis, dim in sides:
        count = lax.axis_size(axis)
        forward = [(i, i + 1) for i in range(count - 1)]
        backward = [(target, source) for source, target in forward]
        low = lax.ppermute(
            lax.slice_in_dim(block, block.shape[dim] - width, None, axis=dim), axis, forward
        )
        high = lax.ppermute(lax.slice_in_dim(block, 0, width, axis=dim), axis, backward)
        block = jnp.concatenate([low, block, high], axis=dim)
    return block


def toeplitz_rows(filter_taps, half_width):
    detectors = filter_taps.shape[0]
    taps_count = filter_taps.shape[1]
    length = 4 * half_width + 1
    widened = jnp.pad(filter_taps, ((0, 0), (0, length - taps_count)))
    tiled = jnp.broadcast_to(widened[:, None, :], (detectors, 2 * half_width, length)).reshape(
        detectors, 2 * half_width * length
    )
    return tiled[:, : 2 * half_width * 4 * half_width].reshape(
        detectors, 2 * half_width, 4 * half_width
    )


def apply_filter(padded, filter_taps, half_width):
    detectors = padded.shape[0]
    blocks = (padded.shape[1] - 2 * half_width) // (2 * half_width)
    pieces = padded.reshape(detectors, blocks + 1, 2 * half_width)
    matrix = toeplitz_rows(filter_taps, half_width)
    lower = jnp.einsum(
        "dbj,dij->dbi", pieces, matrix[:, :, : 2 * half_width], preferred_element_type=jnp.float32
    )
    upper = jnp.einsum(
        "dbj,dij->dbi", pieces, matrix[:, :, 2 * half_width :], preferred_element_type=jnp.float32
    )
    result = lower[:, :-1] + upper[:, 1:]
    return result.reshape(detectors, blocks * 2 * half_width)


def owner_rows(tile_owner):
    total_tiles = tile_owner.shape[0]
    same_owner = tile_owner[:, None] == tile_owner[None, :]
    earlier = jnp.arange(total_tiles)[None, :] < jnp.arange(total_tiles)[:, None]
    slot_rank = jnp.sum((same_owner & earlier).astype(jnp.int32), axis=1)
    return tile_owner * TILE_DEV + slot_rank


def project(summed, left_weight, right_weight):
    tiles_here = summed.shape[0]
    frame_cube = summed.reshape(tiles_here, left_weight.shape[1], right_weight.shape[1])
    partial_value = jnp.einsum(
        "naf,jf->naj", frame_cube, right_weight, precision=lax.Precision.HIGHEST
    )
    result = jnp.einsum("ia,naj->nij", left_weight, partial_value, precision=lax.Precision.HIGHEST)
    return result.reshape(tiles_here, left_weight.shape[0] * right_weight.shape[0])


def local(
    time_stream,
    filter_taps,
    det_precision,
    left_weight,
    right_weight,
    frame_tile,
    tile_owner,
    frame_count,
):
    padded = with_halo(time_stream, (("tm", 1),), HW)
    filtered = apply_filter(padded, filter_taps, HW).astype(jnp.bfloat16)
    regrouped = lax.all_to_all(filtered, "det", split_axis=1, concat_axis=0, tiled=True)
    frame_height = left_weight.shape[1]
    frame_length = right_weight.shape[1]
    detectors_all = det_precision.shape[0]
    groups = detectors_all // frame_height
    columns = regrouped.shape[1] // frame_length
    precision_rows = det_precision.reshape(groups, frame_height, detectors_all)
    sample_rows = regrouped.reshape(detectors_all, columns, frame_length)
    frame_cube = jnp.einsum(
        "gak,kcf->gcaf", precision_rows, sample_rows, preferred_element_type=jnp.float32
    ).astype(jnp.bfloat16)
    frames_here = groups * columns
    frame_width = frame_height * frame_length
    frame_matrix = frame_cube.reshape(frames_here, frame_width)
    tiles_all = tile_owner.shape[0]
    capacity = max(2, 3 * frames_here // (2 * tiles_all))
    tile_index = jnp.arange(tiles_all, dtype=jnp.int32)
    alive_mask = jnp.arange(frames_here, dtype=jnp.int32) < frame_count[0]
    on_tile = frame_tile[:, 0][:, None] == tile_index[None, :]
    dest_row = jnp.sum(jnp.where(on_tile, owner_rows(tile_owner)[None, :], 0), axis=1)
    live_hits = (on_tile & alive_mask[:, None]).astype(jnp.int32)
    earlier = jnp.cumsum(live_hits, axis=0) - live_hits
    slot_rank = jnp.sum(jnp.where(on_tile, earlier, 0), axis=1)
    position = jnp.where(alive_mask, dest_row * capacity + slot_rank, tiles_all * capacity)
    slot_ids = jnp.arange(tiles_all * capacity, dtype=jnp.int32)
    placing = (slot_ids[:, None] == position[None, :]).astype(jnp.bfloat16)
    placed = jnp.dot(placing, frame_matrix, preferred_element_type=jnp.float32)
    buffer = placed.astype(jnp.bfloat16).reshape(
        tiles_all // TILE_DEV, TILE_DEV, capacity * frame_width
    )
    received = lax.all_to_all(buffer, ("tm", "det"), split_axis=0, concat_axis=0, tiled=True)
    summed = jnp.sum(
        received.reshape(received.shape[0], received.shape[1], capacity, frame_width),
        axis=(0, 2),
        dtype=jnp.float32,
    )
    return project(summed, left_weight, right_weight)


def solution(mesh):
    return jax.shard_map(
        local,
        mesh=mesh,
        in_specs=(
            P("det", "tm"),
            P("det", None),
            P(),
            P(),
            P(),
            P(("tm", "det"), None),
            P(),
            P(("tm", "det")),
        ),
        out_specs=P(("tm", "det"), None),
        check_vma=False,
    )
```

profile of v0, /device:TPU:0, one launch (start us, length us, event | category | flops | bytes accessed | tf_op | source)
XLA Modules:
  0.0 251.7 jit_solution(17785269901371639772)
XLA Ops:
  0.0 0.0 copy-start
  0.0 4.2 %copy.36 = bf16[128,8192]{0,1:T(8,128)(2,1)} copy(bf16[128,8192]{1,0:T(8,128)(2,1)} %param.8) | data formatting | bytes 4194304 | tf_op args[0]
  4.2 0.7 fusion.16
  5.0 1.3 collective-permute-start.1
  6.3 5.6 %collective-permute-start = (bf16[128,64]{0,1:T(8,128)(2,1)S(1)}, bf16[128,64]{0,1:T(8,128)(2,1)S(1)}, u32[]{:S(2)}, u32[]{:S(2)}) collective-permute-start(bf16[128,64]{0,1:T(8,128)(2,1)S(1)} %get-tuple-element.11), channel_id=1, source_target_pairs={{0,8},{8,16},{16,24},{1,9},{9,17},{17,25},{2,10},{10,18},{18,26},{... | collective-permute-start | bytes 49160 | tf_op jit(solution)/shard_map/ppermute | solution.py:15
  11.9 0.0 copy-done.4
  11.9 4.4 %broadcast_in_dim.23 = bf16[128,128,257]{0,2,1:T(8,128)(2,1)} broadcast(bf16[128,257]{0,1:T(8,128)(2,1)S(1)} %pad.4), dimensions={0,2} | broadcast | bytes 8487168 | tf_op jit(solution)/shard_map/broadcast_in_dim | solution.py:28
  16.3 12.9 %reshape.79 = bf16[128,32896]{0,1:T(8,128)(2,1)} reshape(bf16[128,128,257]{0,2,1:T(8,128)(2,1)} %broadcast_in_dim.23) | data formatting | bytes 16842752 | tf_op jit(solution)/shard_map/reshape | solution.py:28
  29.2 3.4 %slice-done = bf16[128,32768]{0,1:T(8,128)(2,1)S(1)} async-done(((bf16[128,32896]{0,1:T(8,128)(2,1)}), bf16[128,32768]{0,1:T(8,128)(2,1)S(1)}, s32[]{:S(2)}) %slice-start) | async-done | bytes 8388632 | tf_op jit(solution)/shard_map/slice | solution.py:31
  32.6 3.8 %fusion.14 = (bf16[128,128,128]{0,2,1:T(8,128)(2,1)}, bf16[128,128,128]{0,2,1:T(8,128)(2,1)}) fusion(bf16[128,128,256]{0,2,1:T(8,128)(2,1)S(1)} %bitcast.65), kind=kLoop, calls=%fused_computation.33 | loop fusion | bytes 16777216 | tf_op jit(solution)/shard_map/slice | solution.py:45
  36.4 6.6 %copy.48 = bf16[128,128,128]{2,1,0:T(8,128)(2,1)} copy(bf16[128,128,128]{0,2,1:T(8,128)(2,1)} %get-tuple-element.8) | data formatting | bytes 8388608
  43.1 6.7 %copy.49 = bf16[128,128,128]{2,1,0:T(8,128)(2,1)} copy(bf16[128,128,128]{0,2,1:T(8,128)(2,1)} %get-tuple-element.7) | data formatting | bytes 8388608
  49.8 0.0 collective-permute-done.1
  49.8 0.0 collective-permute-done
  49.8 5.2 %pad_maximum_fusion = bf16[128,8320]{0,1:T(8,128)(2,1)S(1)} fusion(bf16[128,64]{0,1:T(8,128)(2,1)S(1)} %collective-permute-done.1, bf16[128,8192]{0,1:T(8,128)(2,1)} %copy.36, bf16[128,64]{0,1:T(8,128)(2,1)S(1)} %collective-permute-done), kind=kLoop, calls=%fused_computation.7 | loop fusion | flops 6389760 | bytes 4259840 | tf_op jit(solution)/shard_map/concatenate | solution.py:19
  55.0 3.1 %fusion.15 = (bf16[128,64,128]{0,2,1:T(8,128)(2,1)}, bf16[128,64,128]{0,2,1:T(8,128)(2,1)}) fusion(bf16[128,65,128]{0,2,1:T(8,128)(2,1)S(1)} %bitcast.66), kind=kLoop, calls=%fused_computation.34 | loop fusion | bytes 8388608 | tf_op jit(solution)/shard_map/slice | solution.py:47
  58.1 4.1 %copy.50 = bf16[128,64,128]{2,1,0:T(8,128)(2,1)} copy(bf16[128,64,128]{0,2,1:T(8,128)(2,1)} %get-tuple-element.10) | data formatting | bytes 4194304
  62.2 4.1 %copy.51 = bf16[128,64,128]{2,1,0:T(8,128)(2,1)} copy(bf16[128,64,128]{0,2,1:T(8,128)(2,1)} %get-tuple-element.9) | data formatting | bytes 4194304
  66.3 5.9 %fusion.17 = f32[128,64,128]{2,1,0:T(8,128)S(1)} fusion(bf16[128,64,128]{2,1,0:T(8,128)(2,1)} %copy.50, bf16[128,128,128]{2,1,0:T(8,128)(2,1)} %copy.48), kind=kOutput, calls=%fused_computation.36 | convolution fusion | flops 268435456 | bytes 10485760 | tf_op jit(solution)/shard_map/dbj,dij->dbi/dot_general | solution.py:41
  72.3 0.0 copy-done.2
  72.3 4.3 %add_convert_fusion = bf16[128,64,128]{2,1,0:T(8,128)(2,1)} fusion(f32[128,64,128]{2,1,0:T(8,128)S(1)} %fusion.17, bf16[128,64,128]{2,1,0:T(8,128)(2,1)S(1)} %copy-done.3, bf16[128,128,128]{2,1,0:T(8,128)(2,1)S(1)} %copy-done.2), kind=kOutput, calls=%fused_computation.4 | convolution fusion | flops 270532608 | bytes 12582912 | tf_op jit(solution)/shard_map/dbj,dij->dbi/dot_general | solution.py:44
  76.6 4.2 %convert_element_type.37 = bf16[128,8,1024]{2,1,0:T(8,128)(2,1)} reshape(bf16[128,64,128]{2,1,0:T(8,128)(2,1)} %add_convert_fusion) | data formatting | bytes 4194304 | tf_op jit(solution)/shard_map/convert_element_type | solution.py:80
  80.7 4.0 %copy.42 = bf16[128,8,1024]{2,0,1:T(8,128)(2,1)} copy(bf16[128,8,1024]{2,1,0:T(8,128)(2,1)} %convert_element_type.37) | data formatting | bytes 4194304 | tf_op jit(solution)/shard_map/convert_element_type | solution.py:80
  84.8 4.7 %all-to-all-start = ((bf16[128,8,1024]{2,0,1:T(8,128)(2,1)}), bf16[128,8,1024]{2,0,1:T(8,128)(2,1)}, u32[]{:S(2)}, u32[]{:S(2)}) async-start(bf16[128,8,1024]{2,0,1:T(8,128)(2,1)} %copy.42), calls=%async_computation | async-start | bytes 4194304 | tf_op jit(solution)/shard_map/all_to_all | solution.py:81
  90.1 18.0 %reduce-window.6 = s32[64,8,128]{2,1,0:T(8,128)S(1)} reduce-window(s32[64,8,128]{2,1,0:T(8,128)S(1)} %fusion.9, s32[]{:T(128)} %constant.5.clone.1), window={size=1x1x128 pad=0_0x0_0x127_0}, to_apply=%region_2.3 | reduce-window | flops 8323072 | bytes 524292 | tf_op jit(solution)/shard_map/reduce-window
  108.2 0.1 slice.38
  108.3 0.1 copy.34
  108.5 0.1 copy.35
  108.6 0.2 convert_reduce_fusion.1
  108.8 0.1 broadcast_add_fusion
  108.9 0.1 select_reduce_fusion
  109.1 6.8 %all-to-all-done = bf16[128,8,1024]{2,0,1:T(8,128)(2,1)} async-done(((bf16[128,8,1024]{2,0,1:T(8,128)(2,1)}), bf16[128,8,1024]{2,0,1:T(8,128)(2,1)}, u32[]{:S(2)}, u32[]{:S(2)}) %all-to-all-start) | async-done | bytes 2097184 | tf_op jit(solution)/shard_map/all_to_all | solution.py:81
  115.9 4.2 %copy.43 = bf16[8,128,1024]{1,0,2:T(8,128)(2,1)} copy(bf16[8,128,1024]{2,1,0:T(8,128)(2,1)} %bitcast.7) | data formatting | bytes 4194304 | tf_op jit(solution)/shard_map/all_to_all | solution.py:81
  120.0 4.2 %reshape.87 = bf16[1024,32,32,1]{0,2,1,3:T(8,128)(2,1)} reshape(bf16[8,128,1024]{1,0,2:T(8,128)(2,1)} %copy.43) | data formatting | bytes 4194304 | tf_op jit(solution)/shard_map/reshape | solution.py:88
  124.2 0.0 copy-done
  124.3 11.9 %convert_bitcast_fusion = bf16[32,32,32,32]{2,3,0,1:T(8,128)(2,1)} fusion(bf16[32,32,1024,1]{2,1,0,3:T(8,128)(2,1)S(1)} %bitcast.64, bf16[1024,32,32,1]{0,2,1,3:T(8,128)(2,1)} %reshape.87), kind=kOutput, calls=%fused_computation | convolution fusion | flops 2148532224 | bytes 6291456 | tf_op jit(solution)/shard_map/gak,kcf->gcaf/dot_general | solution.py:89
  136.1 12.0 %copy.44 = bf16[32,32,32,32]{3,2,1,0:T(8,128)(2,1)} copy(bf16[32,32,32,32]{2,3,0,1:T(8,128)(2,1)} %convert_bitcast_fusion) | data formatting | bytes 4194304 | tf_op jit(solution)/shard_map/convert_element_type | solution.py:91
  148.1 11.3 %reshape.83 = bf16[1024,1024]{1,0:T(8,128)(2,1)S(1)} reshape(bf16[32,32,32,32]{3,2,1,0:T(8,128)(2,1)} %copy.44) | data formatting | bytes 4194304 | tf_op jit(solution)/shard_map/reshape | solution.py:94
  159.4 4.8 %fusion.1 = bf16[1536,1024]{1,0:T(8,128)(2,1)} fusion(bf16[1024,1024]{1,0:T(8,128)(2,1)S(1)} %reshape.83, s32[1024]{0:T(1024)S(1)} %add_select_fusion), kind=kOutput, calls=%fused_computation.5 | convolution fusion | flops 3224371200 | bytes 5246976 | tf_op jit(solution)/shard_map/dot_general | solution.py:107
  164.2 8.5 %reshape.84 = bf16[32,2,24576]{2,1,0:T(2,128)(2,1)} reshape(bf16[1536,1024]{1,0:T(8,128)(2,1)} %fusion.1) | data formatting | bytes 6291456 | tf_op jit(solution)/shard_map/reshape | solution.py:108
  172.7 74.6 %all_to_all.18 = bf16[32,2,24576]{2,1,0:T(2,128)(2,1)S(1)} all-to-all(bf16[32,2,24576]{2,1,0:T(2,128)(2,1)} %reshape.84), channel_id=1, replica_groups=mesh['tm'=4,'det'=8] {'tm','det'}, dimensions={0} | all-to-all | bytes 6291456 | tf_op jit(solution)/shard_map/all_to_all | solution.py:111
  247.2 2.8 %convert_reduce_fusion = f32[2,24576]{1,0:T(2,128)S(1)} fusion(bf16[32,2,24576]{2,1,0:T(2,128)(2,1)S(1)} %all_to_all.18), kind=kLoop, calls=%fused_computation.1 | loop fusion | flops 3096576 | bytes 3342336 | tf_op jit(solution)/shard_map/reduce_sum | solution.py:112
  250.1 0.1 bitcast_reduce_fusion
  250.2 0.1 reshape.85
  250.2 0.2 fusion.12
  250.4 0.4 convolution_bitcast_fusion
  250.8 0.1 copy.45
  250.9 0.8 copy.58
  (23 shorter events, 0.1 us)
Async XLA Ops:
  0.0 124.3 %copy-start = (bf16[1024,1024]{1,0:T(8,128)(2,1)S(1)}, bf16[1024,1024]{1,0:T(8,128)(2,1)}, u32[]{:S(2)}) copy-start(bf16[1024,1024]{1,0:T(8,128)(2,1)} %param.10) | copy-start | bytes 6291460
  0.0 11.9 %copy-start.4 = (bf16[128,129]{0,1:T(8,128)(2,1)S(1)}, bf16[128,129]{0,1:T(8,128)(2,1)}, u32[]{:S(2)}) copy-start(bf16[128,129]{0,1:T(8,128)(2,1)} %param.9) | copy-start | bytes 99076
  5.0 44.8 %collective-permute-start.1 = (bf16[128,64]{0,1:T(8,128)(2,1)S(1)}, bf16[128,64]{0,1:T(8,128)(2,1)S(1)}, u32[]{:S(2)}, u32[]{:S(2)}) collective-permute-start(bf16[128,64]{0,1:T(8,128)(2,1)S(1)} %get-tuple-element.12), channel_id=1, source_target_pairs={{8,0},{16,8},{24,16},{9,1},{17,9},{25,17},{10,2},{18,10},{26,18},{... | collective-permute-start | bytes 49160 | tf_op jit(solution)/shard_map/ppermute | solution.py:18
  6.3 43.5 %collective-permute-start = (bf16[128,64]{0,1:T(8,128)(2,1)S(1)}, bf16[128,64]{0,1:T(8,128)(2,1)S(1)}, u32[]{:S(2)}, u32[]{:S(2)}) collective-permute-start(bf16[128,64]{0,1:T(8,128)(2,1)S(1)} %get-tuple-element.11), channel_id=1, source_target_pairs={{0,8},{8,16},{16,24},{1,9},{9,17},{17,25},{2,10},{10,18},{18,26},{... | collective-permute-start | bytes 49160 | tf_op jit(solution)/shard_map/ppermute | solution.py:15
  29.2 3.4 %slice-start = ((bf16[128,32896]{0,1:T(8,128)(2,1)}), bf16[128,32768]{0,1:T(8,128)(2,1)S(1)}, s32[]{:S(2)}) async-start(bf16[128,32896]{0,1:T(8,128)(2,1)} %reshape.79), calls=%async_computation.2 | async-start | bytes 16777216 | tf_op jit(solution)/shard_map/slice | solution.py:31
  66.3 5.9 %copy-start.2 = (bf16[128,128,128]{2,1,0:T(8,128)(2,1)S(1)}, bf16[128,128,128]{2,1,0:T(8,128)(2,1)}, u32[]{:S(2)}) copy-start(bf16[128,128,128]{2,1,0:T(8,128)(2,1)} %copy.49) | copy-start | bytes 12582916
  66.3 6.0 %copy-start.3 = (bf16[128,64,128]{2,1,0:T(8,128)(2,1)S(1)}, bf16[128,64,128]{2,1,0:T(8,128)(2,1)}, u32[]{:S(2)}) copy-start(bf16[128,64,128]{2,1,0:T(8,128)(2,1)} %copy.51) | copy-start | bytes 6291460
  84.8 5.3 %copy-start.5 = (s32[1024,1]{0,1:T(1,128)S(1)}, s32[1024,1]{0,1:T(1,128)}, u32[]{:S(2)}) copy-start(s32[1024,1]{0,1:T(1,128)} %param.13) | copy-start | bytes 12292
  84.8 23.8 %copy-start.8 = (s32[64]{0:T(128)S(1)}, s32[64]{0:T(128)}, u32[]{:S(2)}) copy-start(s32[64]{0:T(128)} %param.14) | copy-start | bytes 772
  84.8 31.1 %all-to-all-start = ((bf16[128,8,1024]{2,0,1:T(8,128)(2,1)}), bf16[128,8,1024]{2,0,1:T(8,128)(2,1)}, u32[]{:S(2)}, u32[]{:S(2)}) async-start(bf16[128,8,1024]{2,0,1:T(8,128)(2,1)} %copy.42), calls=%async_computation | async-start | bytes 4194304 | tf_op jit(solution)/shard_map/all_to_all | solution.py:81
  172.7 79.0 %copy-start.1 = (bf16[1024,1024]{1,0:T(8,128)(2,1)S(1)}, bf16[1024,1024]{1,0:T(8,128)(2,1)}, u32[]{:S(2)}) copy-start(bf16[1024,1024]{1,0:T(8,128)(2,1)} %param.10) | copy-start | bytes 6291460
  247.2 3.0 %copy-start.6 = (f32[128,32]{0,1:T(8,128)S(1)}, f32[128,32]{0,1:T(8,128)}, u32[]{:S(2)}) copy-start(f32[128,32]{0,1:T(8,128)} %param.12) | copy-start | bytes 49156
  247.2 3.2 %copy-start.7 = (f32[128,32]{0,1:T(8,128)S(1)}, f32[128,32]{0,1:T(8,128)}, u32[]{:S(2)}) copy-start(f32[128,32]{0,1:T(8,128)} %param.11) | copy-start | bytes 49156
where the time goes:
time: 254 us; the launch traced here: 252 us
  local copies, waits for them, and re-layouts  104 us (41%)
  blocking collectives  74.6 us (29%)
  matrix products  27.4 us (11%)
  other arithmetic  26.6 us (10%)
  starting transfers between devices  11.5 us (5%)
  waiting for transfers between devices  6.84 us (3%)
    all_to_all x1, blocking collectives, local(): lax.all_to_all(buffer, ('tm', 'det'), split_axis=0, concat_axis=0, tiled=...  74.6 us
    unnamed x24, local copies, waits for them, and re-layouts  26.7 us
    another operation x3, other arithmetic  18.2 us
    reshape x1, local copies, waits for them, and re-layouts, toeplitz_rows(): jnp.broadcast_to(widened[:, None, :], (detectors, 2 * half_width, length))  12.9 us
    convert_element_type x1, local copies, waits for them, and re-layouts, local(): frame_cube = jnp.einsum('gak,kcf->gcaf', precision_rows, sample_rows, pre...  12 us
    dot_general x1, matrix products, local(): jnp.einsum('gak,kcf->gcaf', precision_rows, sample_rows, preferred_elemen...  11.9 us
    reshape x1, local copies, waits for them, and re-layouts, local(): frame_matrix = frame_cube.reshape(frames_here, frame_width)  11.3 us
    reshape x1, local copies, waits for them, and re-layouts, local(): placed.astype(jnp.bfloat16)  8.46 us
  transfers between devices with their start and end apart: 3, of which 1 were waited for; matrix products, arithmetic and copies ran while one was open for 21% of the time, Pallas kernels for 0%

commit v1 on v0

v1 whole, which is shorter than its diff:
```python
import functools

import jax
import jax.numpy as jnp
from jax import lax
from jax.experimental import pallas as pl
from jax.experimental.pallas import tpu as pltpu
from jax.sharding import PartitionSpec as P

TILE_DEV = 2
LANES = 128
MESH = pl.DeviceIdType.MESH
VMEM = pltpu.VMEM
F32 = jnp.float32
BF16 = jnp.bfloat16


def owner_rows(tile_owner):
    total_tiles = tile_owner.shape[0]
    same_owner = tile_owner[:, None] == tile_owner[None, :]
    earlier = jnp.arange(total_tiles)[None, :] < jnp.arange(total_tiles)[:, None]
    slot_rank = jnp.sum((same_owner & earlier).astype(jnp.int32), axis=1)
    return tile_owner * TILE_DEV + slot_rank


def edge_kernel(n_tm, n_det, first_ref, last_ref, rows_ref, low_ref, high_ref, all_ref, send_sem, recv_sem, halo_send, halo_recv, own_sem):
    tm, det = lax.axis_index("tm"), lax.axis_index("det")
    has_low, has_high = tm > 0, tm < n_tm - 1
    barrier = pltpu.get_barrier_semaphore()
    for step in range(1, n_det):
        pl.semaphore_signal(barrier, inc=1, device_id=(tm, lax.rem(det + step, n_det)), device_id_type=MESH)

    @pl.when(has_low)
    def _():
        pl.semaphore_signal(barrier, inc=1, device_id=(tm - 1, det), device_id_type=MESH)

    @pl.when(has_high)
    def _():
        pl.semaphore_signal(barrier, inc=1, device_id=(tm + 1, det), device_id_type=MESH)

    pl.semaphore_wait(barrier, n_det - 1 + has_low.astype(jnp.int32) + has_high.astype(jnp.int32))
    down = pltpu.make_async_remote_copy(
        src_ref=first_ref, dst_ref=high_ref, send_sem=halo_send.at[0], recv_sem=halo_recv.at[0],
        device_id=(tm - 1, det), device_id_type=MESH)
    up = pltpu.make_async_remote_copy(
        src_ref=last_ref, dst_ref=low_ref, send_sem=halo_send.at[1], recv_sem=halo_recv.at[1],
        device_id=(tm + 1, det), device_id_type=MESH)

    @pl.when(has_low)
    def _():
        down.start()

    @pl.when(has_high)
    def _():
        up.start()

    copies = []
    for step in range(1, n_det):
        copy = pltpu.make_async_remote_copy(
            src_ref=rows_ref, dst_ref=all_ref.at[det], send_sem=send_sem.at[step], recv_sem=recv_sem.at[step],
            device_id=(tm, lax.rem(det + step, n_det)), device_id_type=MESH)
        copy.start()
        copies.append(copy)
    own = pltpu.make_async_copy(rows_ref, all_ref.at[det], own_sem)
    own.start()

    @pl.when(jnp.logical_not(has_low))
    def _():
        low_ref[...] = jnp.zeros_like(low_ref)

    @pl.when(jnp.logical_not(has_high))
    def _():
        high_ref[...] = jnp.zeros_like(high_ref)

    own.wait()
    for copy in copies:
        copy.wait()

    @pl.when(has_low)
    def _():
        down.wait_send()
        up.wait_recv()

    @pl.when(has_high)
    def _():
        up.wait_send()
        down.wait_recv()


def exchange_edges(n_tm, n_det, first, last, rows):
    vmem = pl.BlockSpec(memory_space=VMEM)
    return pl.pallas_call(
        functools.partial(edge_kernel, n_tm, n_det),
        out_shape=(
            jax.ShapeDtypeStruct(last.shape, last.dtype),
            jax.ShapeDtypeStruct(first.shape, first.dtype),
            jax.ShapeDtypeStruct((n_det,) + rows.shape, rows.dtype),
        ),
        in_specs=[vmem] * 3,
        out_specs=(vmem,) * 3,
        scratch_shapes=[
            pltpu.SemaphoreType.DMA((n_det,)),
            pltpu.SemaphoreType.DMA((n_det,)),
            pltpu.SemaphoreType.DMA((2,)),
            pltpu.SemaphoreType.DMA((2,)),
            pltpu.SemaphoreType.DMA,
        ],
        compiler_params=pltpu.CompilerParams(collective_id=0, has_side_effects=True),
        name="edges",
    )(first, last, rows)


def partial_kernel(
    half, fd, ft, tiles,
    x_ref, low_ref, high_ref, taps_ref, rows_ref, prec_ref, out_ref,
    blocks, result, turned, picks, prec, cells, packed,
):
    dets, samples = x_ref.shape
    width = 2 * half
    nblk = samples // width
    padded = blocks.shape[0] // dets - 1
    groups = prec_ref.shape[0] // fd
    columns = samples // ft
    contract = (((1,), (1,)), ((), ()))

    blocks[0:dets, :] = low_ref[...].astype(F32)
    for b in range(nblk):
        blocks[(b + 1) * dets:(b + 2) * dets, :] = x_ref[:, b * width:(b + 1) * width].astype(F32)
    blocks[(nblk + 1) * dets:(nblk + 2) * dets, :] = high_ref[...].astype(F32)
    blocks[(nblk + 2) * dets:, :] = jnp.zeros((blocks.shape[0] - (nblk + 2) * dets, width), F32)

    rows = jnp.concatenate([rows_ref[s] for s in range(rows_ref.shape[0])], axis=1)
    tile = lax.broadcasted_iota(jnp.int32, (tiles, columns), 0)
    for g in range(groups):
        picks[g * tiles:(g + 1) * tiles, :] = jnp.where(tile == rows[g:g + 1, :], 1.0, 0.0).astype(BF16)
        prec[:, g * dets:(g + 1) * dets] = prec_ref[g * fd:(g + 1) * fd, :]

    unroll = 4

    def filter_step(step, carry):
        for k in range(unroll):
            d = step * unroll + k
            spread = jnp.broadcast_to(taps_ref[pl.ds(d, 1), :], (width, 2 * width))
            matrix = pltpu.roll(spread, 0, 1, stride=1, stride_axis=0).astype(BF16)
            lower = blocks[pl.ds(d, padded, stride=dets), :]
            upper = blocks[pl.ds(d + dets, padded, stride=dets), :]
            window = jnp.concatenate([lower, upper], axis=1).astype(BF16)
            result[pl.ds(d, padded, stride=dets), :] = lax.dot_general(
                window, matrix, contract, preferred_element_type=F32)
        return carry

    lax.fori_loop(0, dets // unroll, filter_step, 0)

    def turn_step(b, carry):
        at = pl.multiple_of(b * dets, dets)
        to = pl.multiple_of(b * width, width)
        turned[pl.ds(to, width), :] = result[pl.ds(at, dets), :].T
        return carry

    lax.fori_loop(0, nblk + 1, turn_step, 0)

    share = 4

    def sum_step(pair, carry):
        f = pair * 2
        left = turned[pl.ds(half + f, columns, stride=ft), :]
        right = turned[pl.ds(half + f + 1, columns, stride=ft), :]
        weight = jnp.concatenate([left, right], axis=1).astype(BF16)
        at = pl.multiple_of(f * tiles, tiles)
        for g in range(0, groups, share):
            sums = jnp.dot(picks[g * tiles:(g + share) * tiles, :], weight, preferred_element_type=F32).astype(BF16)
            for k in range(share):
                for side in range(2):
                    cells[pl.ds(at + side * tiles, tiles), (g + k) * dets:(g + k + 1) * dets] = (
                        sums[k * tiles:(k + 1) * tiles, side * dets:(side + 1) * dets])
        return carry

    lax.fori_loop(0, ft // 2, sum_step, 0)

    across = LANES // fd
    low = ft // across

    def product_step(u, carry):
        parts = []
        for v in range(across):
            at = pl.multiple_of((v * low + u) * tiles, tiles)
            parts.append(lax.dot_general(cells[pl.ds(at, tiles), :], prec[...], contract, preferred_element_type=F32))
        packed[pl.ds(pl.multiple_of(u * tiles, tiles), tiles), :] = jnp.concatenate(parts, axis=1)
        return carry

    lax.fori_loop(0, low, product_step, 0)
    for owner in range(out_ref.shape[0]):
        mine = [packed[pl.ds(owner * TILE_DEV + k, low, stride=tiles), :] for k in range(TILE_DEV)]
        out_ref[owner] = jnp.concatenate(mine, axis=0).astype(out_ref.dtype)


def partial_sums(x, low, high, taps, rows, precision, half, fd, ft, tiles):
    dets, samples = x.shape
    width = 2 * half
    padded = -(-(samples // width + 1) // 8) * 8
    groups = precision.shape[0] // fd
    widened = jnp.pad(taps.astype(F32), ((0, 0), (0, 2 * width - taps.shape[1])))
    vmem = pl.BlockSpec(memory_space=VMEM)
    across = LANES // fd
    return pl.pallas_call(
        functools.partial(partial_kernel, half, fd, ft, tiles),
        out_shape=jax.ShapeDtypeStruct((tiles // TILE_DEV, TILE_DEV * ft // across, LANES), BF16),
        in_specs=[vmem] * 6,
        out_specs=vmem,
        scratch_shapes=[
            VMEM(((padded + 1) * dets, width), F32),
            VMEM((padded * dets, width), F32),
            VMEM((samples + width, dets), F32),
            VMEM((groups * tiles, samples // ft), BF16),
            VMEM((fd, groups * dets), BF16),
            VMEM((ft * tiles, groups * dets), BF16),
            VMEM((ft // across * tiles, LANES), F32),
        ],
        compiler_params=pltpu.CompilerParams(vmem_limit_bytes=60 * 1024 * 1024),
        name="partials",
    )(x, low, high, widened, rows, precision)


def plain_partial_sums(x, low, high, taps, rows, precision, half, fd, ft, tiles):
    dets, samples = x.shape
    width = 2 * half
    groups = precision.shape[0] // fd
    blocks = samples // width
    padded = jnp.concatenate([low[:, -half:], x, high[:, :half]], axis=1).reshape(dets, blocks + 1, width)
    length = 4 * half + 1
    tiled = jnp.broadcast_to(jnp.pad(taps, ((0, 0), (0, length - taps.shape[1])))[:, None, :], (dets, width, length))
    matrix = tiled.reshape(dets, width * length)[:, :width * 2 * width].reshape(dets, width, 2 * width)
    near = jnp.einsum("dbj,dij->dbi", padded, matrix[:, :, :width], preferred_element_type=F32)
    far = jnp.einsum("dbj,dij->dbi", padded, matrix[:, :, width:], preferred_element_type=F32)
    filtered = (near[:, :-1] + far[:, 1:]).astype(BF16).reshape(dets, samples // ft, ft)
    picks = (rows.transpose(1, 0, 2).reshape(groups, 1, -1) == jnp.arange(tiles, dtype=jnp.int32)[None, :, None]).astype(BF16)
    sums = jnp.einsum("gkt,dtf->gkfd", picks, filtered, preferred_element_type=F32).astype(BF16)
    out = jnp.einsum("gkfd,gad->kfa", sums, precision.reshape(groups, fd, dets), preferred_element_type=F32)
    across = LANES // fd
    low_part = ft // across
    out = out.reshape(tiles, across, low_part, fd).transpose(0, 2, 1, 3)
    return out.reshape(tiles // TILE_DEV, TILE_DEV * low_part, LANES).astype(BF16)


def gather_kernel(n_tm, n_det, part_ref, left_ref, right_ref, out_ref, held, send_sem, recv_sem, own_sem):
    tm, det = lax.axis_index("tm"), lax.axis_index("det")
    count = n_tm * n_det
    me = tm * n_det + det
    fd = left_ref.shape[0]
    barrier = pltpu.get_barrier_semaphore()

    def peer(step):
        other = lax.rem(me + step, count)
        return other, (other // n_det, lax.rem(other, n_det))

    for step in range(1, count):
        pl.semaphore_signal(barrier, inc=1, device_id=peer(step)[1], device_id_type=MESH)
    own = pltpu.make_async_copy(part_ref.at[me], held.at[me], own_sem)
    own.start()
    pl.semaphore_wait(barrier, count - 1)
    copies = []
    for step in range(1, count):
        other, where = peer(step)
        copy = pltpu.make_async_remote_copy(
            src_ref=part_ref.at[other], dst_ref=held.at[me], send_sem=send_sem.at[step], recv_sem=recv_sem.at[step],
            device_id=where, device_id_type=MESH)
        copy.start()
        copies.append(copy)
    own.wait()
    for copy in copies:
        copy.wait()
    total = jnp.sum(held[...].astype(F32), axis=0)
    low = total.shape[0] // TILE_DEV
    across = total.shape[1] // fd
    for k in range(TILE_DEV):
        tile = total[k * low:(k + 1) * low, :]
        stacked = jnp.concatenate([tile[:, v * fd:(v + 1) * fd] for v in range(across)], axis=0)
        rows = jnp.dot(stacked, left_ref[...], precision=lax.Precision.HIGHEST, preferred_element_type=F32)
        out_ref[k] = lax.dot_general(
            rows, right_ref[...], (((0,), (0,)), ((), ())), precision=lax.Precision.HIGHEST,
            preferred_element_type=F32)


def gather_tiles(n_tm, n_det, part, left, right):
    count = n_tm * n_det
    vmem = pl.BlockSpec(memory_space=VMEM)
    return pl.pallas_call(
        functools.partial(gather_kernel, n_tm, n_det),
        out_shape=jax.ShapeDtypeStruct((TILE_DEV, left.shape[1], right.shape[1]), F32),
        in_specs=[vmem] * 3,
        out_specs=vmem,
        scratch_shapes=[
            VMEM(part.shape, part.dtype),
            pltpu.SemaphoreType.DMA((count,)),
            pltpu.SemaphoreType.DMA((count,)),
            pltpu.SemaphoreType.DMA,
        ],
        compiler_params=pltpu.CompilerParams(collective_id=1, has_side_effects=True),
        name="gather",
    )(part, left, right)


def local(
    n_tm, n_det,
    time_stream, filter_taps, det_precision, left_weight, right_weight, frame_tile, tile_owner, frame_count,
):
    half = filter_taps.shape[1] // 2
    width = 2 * half
    fd, ft = left_weight.shape[1], right_weight.shape[1]
    dets = time_stream.shape[0]
    tiles = tile_owner.shape[0]
    frames = frame_tile.shape[0]
    groups = det_precision.shape[0] // fd
    on_tile = frame_tile == jnp.arange(tiles, dtype=jnp.int32)[None, :]
    dest_row = jnp.sum(jnp.where(on_tile, owner_rows(tile_owner)[None, :], 0), axis=1)
    alive = jnp.arange(frames, dtype=jnp.int32) < frame_count[0]
    rows = jnp.where(alive, dest_row, -1).reshape(groups, frames // groups)
    low, high, rows = exchange_edges(n_tm, n_det, time_stream[:, :width], time_stream[:, -width:], rows)
    precision = lax.dynamic_slice_in_dim(det_precision, lax.axis_index("det") * dets, dets, axis=1)
    form = partial_sums if dets % LANES == 0 else plain_partial_sums
    part = form(time_stream, low, high, filter_taps, rows, precision, half, fd, ft, tiles)
    sky = gather_tiles(n_tm, n_det, part, left_weight.T, right_weight.T)
    return sky.reshape(TILE_DEV, -1)


def solution(mesh):
    return jax.shard_map(
        functools.partial(local, mesh.shape["tm"], mesh.shape["det"]),
        mesh=mesh,
        in_specs=(
            P("det", "tm"),
            P("det", None),
            P(),
            P(),
            P(),
            P(("tm", "det"), None),
            P(),
            P(("tm", "det")),
        ),
        out_specs=P(("tm", "det"), None),
        check_vma=False,
    )
```

time: 254 us -> 66.3 us (0.26)
  local copies, waits for them, and re-layouts: 104 us -> 4.76 us
  blocking collectives: 74.6 us -> 0 us
  Pallas kernels: 0 us -> 56.6 us
  matrix products: 27.4 us -> 0 us
  other arithmetic: 26.6 us -> 3.64 us
  starting transfers between devices: 11.5 us -> 0 us
  waiting for transfers between devices: 6.84 us -> 0 us
    all_to_all x1 -> x0, blocking collectives: 74.6 us -> none  [local(): lax.all_to_all(buffer, ('tm', 'det'), split_axis=0, concat_axis=0, tiled=...]
    pallas_call x0 -> x3, Pallas kernels: none -> 56.6 us  [the longest x1 36.8 us: partial_sums(): pl.pallas_call(functools.partial(partial_kernel, half, fd, ft, tiles), ou...]
    reshape x5 -> x0, local copies, waits for them, and re-layouts: 37 us -> none  [the longest x1 12.9 us: toeplitz_rows(): jnp.broadcast_to(widened[:, None, :], (detectors, 2 * half_width, length))]
    dot_general x6 -> x0, matrix products: 27.4 us -> none  [the longest x1 11.9 us: local(): jnp.einsum('gak,kcf->gcaf', precision_rows, sample_rows, preferred_elemen...]
    unnamed x24 -> x4, local copies, waits for them, and re-layouts: 26.7 us -> 2.52 us
    convert_element_type x3 -> x0, local copies, waits for them, and re-layouts: 20.2 us -> none  [the longest x1 12 us: local(): frame_cube = jnp.einsum('gak,kcf->gcaf', precision_rows, sample_rows, pre...]
    another operation x3 -> x0, other arithmetic: 18.2 us -> none
    slice x7 -> x1, local copies, waits for them, and re-layouts: 11.3 us -> 1.4 us  [local(): time_stream[:, -width:]]
  transfers between devices with their start and end apart: 3 -> 0, of which waited for: 1 -> 0; matrix products, arithmetic and copies ran while one was open for 21% -> 0% of each run, Pallas kernels for 0% -> 0%
where the time goes in v1:
time: 66.3 us; the launch traced here: 65.9 us
  Pallas kernels  56.6 us (85%)
  local copies, waits for them, and re-layouts  4.76 us (7%)
  other arithmetic  3.64 us (5%)
  between operations  0.85 us (1%)
    pallas_call x1, Pallas kernels, partial_sums(): pl.pallas_call(functools.partial(partial_kernel, half, fd, ft, tiles), ou...  36.8 us
    pallas_call x1, Pallas kernels, gather_tiles(): pl.pallas_call(functools.partial(gather_kernel, n_tm, n_det), out_shape=j...  10.8 us
    pallas_call x1, Pallas kernels, exchange_edges(): pl.pallas_call(functools.partial(edge_kernel, n_tm, n_det), out_shape=(ja...  9.03 us
    unnamed x4, local copies, waits for them, and re-layouts  2.52 us
    slice x1, local copies, waits for them, and re-layouts, local(): time_stream[:, -width:]  1.4 us

profile of v1, /device:TPU:0, one launch (start us, length us, event | category | flops | bytes accessed | tf_op | source)
XLA Modules:
  0.0 65.9 jit_solution(17929657003194205653)
XLA Ops:
  0.0 0.0 copy-start
  0.8 0.9 %convert_reduce_fusion = s32[64]{0:T(128)S(1)} fusion(s32[64]{0:T(128)} %param.14), kind=kLoop, calls=%fused_computation.4 | loop fusion | flops 20416 | bytes 512 | tf_op jit(solution)/shard_map/reduce_sum | solution.py:22
  1.7 0.7 %multiply_add_fusion = s32[64]{0:T(128)S(1)} fusion(s32[64]{0:T(128)S(1)} %convert_reduce_fusion, s32[64]{0:T(128)} %param.14), kind=kLoop, calls=%fused_computation.9 | loop fusion | flops 128 | bytes 768 | tf_op jit(solution)/shard_map/add | solution.py:23
  2.4 0.8 %select_reduce_fusion = s32[1024]{0:T(1024)S(1)} fusion(s32[64]{0:T(128)S(1)} %multiply_add_fusion, s32[1024]{0:T(1024)} %bitcast.12), kind=kLoop, calls=%fused_computation | loop fusion | flops 195584 | bytes 8448 | tf_op jit(solution)/shard_map/reduce_sum | solution.py:315
  3.2 0.1 reduce_sum.22
  3.2 0.6 fusion.1.rows_ref
  3.9 0.9 %copy.10 = bf16[128,129]{1,0:T(8,128)(2,1)S(1)} copy(bf16[128,129]{0,1:T(8,128)(2,1)} %param.9) | data formatting | bytes 66048 | tf_op args[1]
  4.7 0.7 %pad_convert_fusion.taps_ref = f32[128,256]{1,0:T(8,128)} fusion(bf16[128,129]{1,0:T(8,128)(2,1)S(1)} %copy.10), kind=kLoop, calls=%fused_computation.3 | loop fusion | flops 32768 | bytes 164096 | tf_op jit(solution)/shard_map/jit(_pad)/pad | solution.py:202
  5.4 1.4 %fusion.2 = (bf16[128,128]{1,0:T(8,128)(2,1)}, bf16[128,128]{1,0:T(8,128)(2,1)}) fusion(bf16[128,8192]{1,0:T(8,128)(2,1)} %x_ref.1), kind=kLoop, calls=%fused_computation.11 | loop fusion | bytes 131072 | tf_op jit(solution)/shard_map/slice | solution.py:318
  6.8 9.0 %edges.1 = (bf16[128,128]{1,0:T(8,128)(2,1)}, bf16[128,128]{1,0:T(8,128)(2,1)}, s32[8,32,32]{2,1,0:T(8,128)}) custom-call(bf16[128,128]{1,0:T(8,128)(2,1)} %get-tuple-element.12.first_ref, bf16[128,128]{1,0:T(8,128)(2,1)} %get-tuple-element.11.last_ref, s32[32,32]{1,0:T(8,128)} %fusion.1.rows_ref), custom_call_target="tpu_custom_call" | custom-call | tf_op jit(solution)/shard_map/edges/pallas_call | solution.py:92
  15.8 0.0 copy-done
  15.8 0.8 %constant_dynamic-slice_fusion.prec_ref = bf16[1024,128]{1,0:T(8,128)(2,1)} fusion(bf16[1024,1024]{1,0:T(8,128)(2,1)S(1)} %copy-done, s32[]{:T(128)S(6)} %select_n.14), kind=kLoop, calls=%fused_computation.10 | loop fusion | bytes 524292 | tf_op jit(solution)/shard_map/dynamic_slice | solution.py:319
  16.6 36.8 %partials.1.part_ref = bf16[32,16,128]{2,1,0:T(8,128)(2,1)} custom-call(bf16[128,8192]{1,0:T(8,128)(2,1)} %x_ref.1, bf16[128,128]{1,0:T(8,128)(2,1)} %get-tuple-element.8.low_ref, bf16[128,128]{1,0:T(8,128)(2,1)} %get-tuple-element.9.high_ref, f32[128,256]{1,0:T(8,128)} %pad_convert_fusion.taps_ref, s32[8,32,32]{2,1,0:T(8,128)} %get-tuple-element.10.rows_ref, ...), custom_call_target="tpu_custom_call" | custom-call | tf_op jit(solution)/shard_map/partials/pallas_call | solution.py:205
  53.4 10.8 %gather.1 = f32[2,128,128]{2,1,0:T(8,128)} custom-call(bf16[32,16,128]{2,1,0:T(8,128)(2,1)} %partials.1.part_ref, f32[32,128]{1,0:T(8,128)} %bitcast.10, f32[32,128]{1,0:T(8,128)} %bitcast.11), custom_call_target="tpu_custom_call" | custom-call | tf_op jit(solution)/shard_map/gather/pallas_call | solution.py:287
  64.2 1.7 %copy.13 = f32[1,2,128,128]{3,1,2,0:T(2,128)} copy(f32[1,2,128,128]{3,2,1,0:T(8,128)} %bitcast.9) | data formatting | bytes 262144
Async XLA Ops:
  0.0 15.8 %copy-start = (bf16[1024,1024]{1,0:T(8,128)(2,1)S(1)}, bf16[1024,1024]{1,0:T(8,128)(2,1)}, u32[]{:S(2)}) copy-start(bf16[1024,1024]{1,0:T(8,128)(2,1)} %param.10) | copy-start | bytes 6291460

commit v2 on v1

v2 whole, which is shorter than its diff:
```python
import functools

import jax
import jax.numpy as jnp
from jax import lax
from jax.experimental import pallas as pl
from jax.experimental.pallas import tpu as pltpu
from jax.sharding import PartitionSpec as P

TILE_DEV = 2
LANES = 128
MESH = pl.DeviceIdType.MESH
VMEM = pltpu.VMEM
F32 = jnp.float32
BF16 = jnp.bfloat16


def owner_rows(tile_owner):
    total_tiles = tile_owner.shape[0]
    same_owner = tile_owner[:, None] == tile_owner[None, :]
    earlier = jnp.arange(total_tiles)[None, :] < jnp.arange(total_tiles)[:, None]
    slot_rank = jnp.sum((same_owner & earlier).astype(jnp.int32), axis=1)
    return tile_owner * TILE_DEV + slot_rank


def edge_kernel(n_tm, n_det, width, x_ref, tile_ref, count_ref, low_ref, high_ref, all_ref, rows_ref, send_sem, recv_sem, halo_send, halo_recv, own_sem):
    tm, det = lax.axis_index("tm"), lax.axis_index("det")
    has_low, has_high = tm > 0, tm < n_tm - 1
    barrier = pltpu.get_barrier_semaphore()
    for step in range(1, n_det):
        pl.semaphore_signal(barrier, inc=1, device_id=(tm, lax.rem(det + step, n_det)), device_id_type=MESH)

    @pl.when(has_low)
    def _():
        pl.semaphore_signal(barrier, inc=1, device_id=(tm - 1, det), device_id_type=MESH)

    @pl.when(has_high)
    def _():
        pl.semaphore_signal(barrier, inc=1, device_id=(tm + 1, det), device_id_type=MESH)

    tile = tile_ref[...]
    frame = lax.broadcasted_iota(jnp.int32, tile.shape, 0) * tile.shape[1] + lax.broadcasted_iota(jnp.int32, tile.shape, 1)
    rows_ref[...] = jnp.where(frame < count_ref[0], tile, -1)
    pl.semaphore_wait(barrier, n_det - 1 + has_low.astype(jnp.int32) + has_high.astype(jnp.int32))
    down = pltpu.make_async_remote_copy(
        src_ref=x_ref.at[:, 0:width], dst_ref=high_ref, send_sem=halo_send.at[0], recv_sem=halo_recv.at[0],
        device_id=(tm - 1, det), device_id_type=MESH)
    up = pltpu.make_async_remote_copy(
        src_ref=x_ref.at[:, x_ref.shape[1] - width:], dst_ref=low_ref, send_sem=halo_send.at[1], recv_sem=halo_recv.at[1],
        device_id=(tm + 1, det), device_id_type=MESH)

    @pl.when(has_low)
    def _():
        down.start()

    @pl.when(has_high)
    def _():
        up.start()

    copies = []
    for step in range(1, n_det):
        copy = pltpu.make_async_remote_copy(
            src_ref=rows_ref, dst_ref=all_ref.at[det], send_sem=send_sem.at[step], recv_sem=recv_sem.at[step],
            device_id=(tm, lax.rem(det + step, n_det)), device_id_type=MESH)
        copy.start()
        copies.append(copy)
    own = pltpu.make_async_copy(rows_ref, all_ref.at[det], own_sem)
    own.start()

    @pl.when(jnp.logical_not(has_low))
    def _():
        low_ref[...] = jnp.zeros_like(low_ref)

    @pl.when(jnp.logical_not(has_high))
    def _():
        high_ref[...] = jnp.zeros_like(high_ref)

    own.wait()
    for copy in copies:
        copy.wait()

    @pl.when(has_low)
    def _():
        down.wait_send()
        up.wait_recv()

    @pl.when(has_high)
    def _():
        up.wait_send()
        down.wait_recv()


def exchange_edges(n_tm, n_det, width, x, tile, count):
    vmem = pl.BlockSpec(memory_space=VMEM)
    halo = jax.ShapeDtypeStruct((x.shape[0], width), x.dtype)
    return pl.pallas_call(
        functools.partial(edge_kernel, n_tm, n_det, width),
        out_shape=(halo, halo, jax.ShapeDtypeStruct((n_det,) + tile.shape, tile.dtype)),
        in_specs=[pl.BlockSpec(memory_space=pl.ANY), vmem, pl.BlockSpec(memory_space=pltpu.SMEM)],
        out_specs=(vmem,) * 3,
        scratch_shapes=[
            VMEM(tile.shape, tile.dtype),
            pltpu.SemaphoreType.DMA((n_det,)),
            pltpu.SemaphoreType.DMA((n_det,)),
            pltpu.SemaphoreType.DMA((2,)),
            pltpu.SemaphoreType.DMA((2,)),
            pltpu.SemaphoreType.DMA,
        ],
        compiler_params=pltpu.CompilerParams(collective_id=0, has_side_effects=True),
        name="edges",
    )(x, tile, count)


def divisor(number, most):
    return max(d for d in range(1, most + 1) if number % d == 0)


def partial_body(
    half, fd, ft, tiles,
    x_ref, low_ref, high_ref, tapst_ref, rows_ref, owner_ref, prec_ref, out_ref,
    wide, taps_ref, blocks, result, turned, picks, prec, cells, packed,
):
    dets, samples = x_ref.shape
    width = 2 * half
    nblk = samples // width
    padded = blocks.shape[0] // dets - 1
    groups = prec_ref.shape[0] // fd
    columns = samples // ft
    contract = (((1,), (1,)), ((), ()))

    blocks[0:dets, :] = low_ref[...].astype(F32)
    for b in range(nblk):
        blocks[(b + 1) * dets:(b + 2) * dets, :] = x_ref[:, b * width:(b + 1) * width].astype(F32)
    blocks[(nblk + 1) * dets:(nblk + 2) * dets, :] = high_ref[...].astype(F32)
    blocks[(nblk + 2) * dets:, :] = jnp.zeros((blocks.shape[0] - (nblk + 2) * dets, width), F32)

    wide[...] = jnp.zeros(wide.shape, F32)
    wide[0:tapst_ref.shape[0], :] = tapst_ref[...].astype(F32)
    taps_ref[...] = wide[...].T

    across_owner = jnp.broadcast_to(owner_ref[...].astype(F32), (tiles, tiles))
    down = lax.broadcasted_iota(jnp.int32, (tiles, tiles), 0)
    across_tile = lax.broadcasted_iota(jnp.int32, (tiles, tiles), 1)
    earlier = (across_owner.T == across_owner) & (down < across_tile)
    rank = jnp.sum(jnp.where(earlier, 1.0, 0.0), axis=0, keepdims=True)
    place = across_owner * TILE_DEV + rank
    order = jnp.sum(jnp.where(place == down.astype(F32), across_tile.astype(F32), 0.0), axis=1, keepdims=True)
    order = jnp.broadcast_to(order, (tiles, columns))
    per_row = rows_ref.shape[2] // (columns // rows_ref.shape[0])
    span = rows_ref.shape[2] // per_row
    for q in range(per_row):
        rows = jnp.concatenate([rows_ref[s][:, q * span:(q + 1) * span] for s in range(rows_ref.shape[0])], axis=1).astype(F32)
        for r in range(rows.shape[0]):
            g = r * per_row + q
            picks[g * tiles:(g + 1) * tiles, :] = jnp.where(order == rows[r:r + 1, :], 1.0, 0.0).astype(BF16)
    for g in range(groups):
        prec[:, g * dets:(g + 1) * dets] = prec_ref[g * fd:(g + 1) * fd, :]

    unroll = divisor(dets, 16)

    def filter_step(step, carry):
        for k in range(unroll):
            d = step * unroll + k
            spread = jnp.broadcast_to(taps_ref[pl.ds(d, 1), :], (width, 2 * width))
            matrix = pltpu.roll(spread, 0, 1, stride=1, stride_axis=0).astype(BF16)
            lower = blocks[pl.ds(d, padded, stride=dets), :]
            upper = blocks[pl.ds(d + dets, padded, stride=dets), :]
            window = jnp.concatenate([lower, upper], axis=1).astype(BF16)
            result[pl.ds(d, padded, stride=dets), :] = lax.dot_general(
                window, matrix, contract, preferred_element_type=F32)
        return carry

    lax.fori_loop(0, dets // unroll, filter_step, 0)

    turns = divisor(nblk + 1, 16)

    def turn_step(step, carry):
        for k in range(turns):
            b = step * turns + k
            at = pl.multiple_of(b * dets, dets)
            to = pl.multiple_of(b * width, width)
            turned[pl.ds(to, width), :] = result[pl.ds(at, dets), :].astype(BF16).T.astype(F32)
        return carry

    lax.fori_loop(0, (nblk + 1) // turns, turn_step, 0)

    share = 4

    pairs = divisor(ft // 2, 4)

    def sum_pair(pair):
        f = pair * 2
        left = turned[pl.ds(half + f, columns, stride=ft), :]
        right = turned[pl.ds(half + f + 1, columns, stride=ft), :]
        weight = jnp.concatenate([left, right], axis=1).astype(BF16)
        at = pl.multiple_of(f * tiles, tiles)
        for g in range(0, groups, share):
            sums = jnp.dot(picks[g * tiles:(g + share) * tiles, :], weight, preferred_element_type=F32).astype(BF16)
            for k in range(share):
                for side in range(2):
                    cells[pl.ds(at + side * tiles, tiles), (g + k) * dets:(g + k + 1) * dets] = (
                        sums[k * tiles:(k + 1) * tiles, side * dets:(side + 1) * dets])

    def sum_step(step, carry):
        for k in range(pairs):
            sum_pair(step * pairs + k)
        return carry

    lax.fori_loop(0, ft // 2 // pairs, sum_step, 0)

    across = LANES // fd
    low = ft // across

    def product_step(u, carry):
        parts = []
        for v in range(across):
            at = pl.multiple_of((v * low + u) * tiles, tiles)
            parts.append(lax.dot_general(cells[pl.ds(at, tiles), :], prec[...], contract, preferred_element_type=F32))
        packed[pl.ds(pl.multiple_of(u * tiles, tiles), tiles), :] = jnp.concatenate(parts, axis=1)
        return carry

    lax.fori_loop(0, low, product_step, 0, unroll=2)
    for owner in range(out_ref.shape[0]):
        mine = [packed[pl.ds(owner * TILE_DEV + k, low, stride=tiles), :] for k in range(TILE_DEV)]
        out_ref[owner] = jnp.concatenate(mine, axis=0).astype(out_ref.dtype)


def partial_scratch(half, fd, ft, tiles, x, precision):
    dets, samples = x.shape
    width = 2 * half
    padded = -(-(samples // width + 1) // 8) * 8
    groups = precision.shape[0] // fd
    across = LANES // fd
    return [
        VMEM((2 * width, dets), F32),
        VMEM((dets, 2 * width), F32),
        VMEM(((padded + 1) * dets, width), F32),
        VMEM((padded * dets, width), F32),
        VMEM((samples + width, dets), F32),
        VMEM((groups * tiles, samples // ft), BF16),
        VMEM((fd, groups * dets), BF16),
        VMEM((ft * tiles, groups * dets), BF16),
        VMEM((ft // across * tiles, LANES), F32),
    ]


def part_shape(fd, ft, tiles):
    return (tiles // TILE_DEV, TILE_DEV * ft // (LANES // fd), LANES)


def plain_partial_sums(x, low, high, taps, rows, owner, precision, half, fd, ft, tiles):
    dets, samples = x.shape
    width = 2 * half
    groups = precision.shape[0] // fd
    blocks = samples // width
    padded = jnp.concatenate([low[:, -half:], x, high[:, :half]], axis=1).reshape(dets, blocks + 1, width)
    length = 4 * half + 1
    tiled = jnp.broadcast_to(jnp.pad(taps, ((0, 0), (0, length - taps.shape[1])))[:, None, :], (dets, width, length))
    matrix = tiled.reshape(dets, width * length)[:, :width * 2 * width].reshape(dets, width, 2 * width)
    near = jnp.einsum("dbj,dij->dbi", padded, matrix[:, :, :width], preferred_element_type=F32)
    far = jnp.einsum("dbj,dij->dbi", padded, matrix[:, :, width:], preferred_element_type=F32)
    filtered = (near[:, :-1] + far[:, 1:]).astype(BF16).reshape(dets, samples // ft, ft)
    order = jnp.argsort(owner_rows(owner)).astype(jnp.int32)
    rows = rows.reshape(rows.shape[0], groups, -1).transpose(1, 0, 2).reshape(groups, 1, -1)
    picks = (rows == order[None, :, None]).astype(BF16)
    sums = jnp.einsum("gkt,dtf->gkfd", picks, filtered, preferred_element_type=F32).astype(BF16)
    out = jnp.einsum("gkfd,gad->kfa", sums, precision.reshape(groups, fd, dets), preferred_element_type=F32)
    across = LANES // fd
    low_part = ft // across
    out = out.reshape(tiles, across, low_part, fd).transpose(0, 2, 1, 3)
    return out.reshape(tiles // TILE_DEV, TILE_DEV * low_part, LANES).astype(BF16)


def peer(me, step, n_tm, n_det):
    other = lax.rem(me + step, n_tm * n_det)
    return other, (other // n_det, lax.rem(other, n_det))


def greet(n_tm, n_det):
    me = lax.axis_index("tm") * n_det + lax.axis_index("det")
    barrier = pltpu.get_barrier_semaphore()
    for step in range(1, n_tm * n_det):
        pl.semaphore_signal(barrier, inc=1, device_id=peer(me, step, n_tm, n_det)[1], device_id_type=MESH)
    return me, barrier


def gather_body(n_tm, n_det, me, barrier, part_ref, left_ref, right_ref, out_ref, held, send_sem, recv_sem, own_sem):
    count = n_tm * n_det
    fd = left_ref.shape[0]
    pl.semaphore_wait(barrier, count - 1)
    copies = []
    for step in range(1, count):
        other, where = peer(me, step, n_tm, n_det)
        copy = pltpu.make_async_remote_copy(
            src_ref=part_ref.at[other], dst_ref=held.at[me], send_sem=send_sem.at[step], recv_sem=recv_sem.at[step],
            device_id=where, device_id_type=MESH)
        copy.start()
        copies.append(copy)
    own = pltpu.make_async_copy(part_ref.at[me], held.at[me], own_sem)
    own.start()
    own.wait()
    for copy in copies:
        copy.wait()
    total = jnp.sum(held[...].astype(F32), axis=0)
    low = total.shape[0] // TILE_DEV
    across = total.shape[1] // fd
    for k in range(TILE_DEV):
        tile = total[k * low:(k + 1) * low, :]
        stacked = jnp.concatenate([tile[:, v * fd:(v + 1) * fd] for v in range(across)], axis=0)
        rows = jnp.dot(stacked, left_ref[...], precision=lax.Precision.HIGHEST, preferred_element_type=F32)
        out_ref[k] = lax.dot_general(
            rows, right_ref[...], (((0,), (0,)), ((), ())), precision=lax.Precision.HIGHEST,
            preferred_element_type=F32)


def gather_kernel(n_tm, n_det, part_ref, left_ref, right_ref, out_ref, *scratch):
    me, barrier = greet(n_tm, n_det)
    gather_body(n_tm, n_det, me, barrier, part_ref, left_ref, right_ref, out_ref, *scratch)


def whole_kernel(n_tm, n_det, sizes, *refs):
    ins, (left_ref, right_ref, out_ref, part), rest = refs[:7], refs[7:11], refs[11:]
    me, barrier = greet(n_tm, n_det)
    partial_body(*sizes, *ins, part, *rest[:-4])
    gather_body(n_tm, n_det, me, barrier, part, left_ref, right_ref, out_ref, *rest[-4:])


def gather_scratch(count, shape):
    return [
        VMEM(shape, BF16),
        pltpu.SemaphoreType.DMA((count,)),
        pltpu.SemaphoreType.DMA((count,)),
        pltpu.SemaphoreType.DMA,
    ]


def call(kernel, inputs, scratch, tall, name):
    vmem = pl.BlockSpec(memory_space=VMEM)
    return pl.pallas_call(
        kernel,
        out_shape=jax.ShapeDtypeStruct((TILE_DEV,) + tall, F32),
        in_specs=[vmem] * len(inputs),
        out_specs=vmem,
        scratch_shapes=scratch,
        compiler_params=pltpu.CompilerParams(
            collective_id=1, has_side_effects=True, vmem_limit_bytes=60 * 1024 * 1024),
        name=name,
    )(*inputs)


def local(
    n_tm, n_det,
    time_stream, filter_taps, det_precision, left_weight, right_weight, frame_tile, tile_owner, frame_count,
):
    half = filter_taps.shape[1] // 2
    fd, ft = left_weight.shape[1], right_weight.shape[1]
    dets = time_stream.shape[0]
    tiles = tile_owner.shape[0]
    count = n_tm * n_det
    low, high, rows = exchange_edges(n_tm, n_det, 2 * half, time_stream, frame_tile.reshape(-1, LANES), frame_count)
    precision = lax.dynamic_slice_in_dim(det_precision, lax.axis_index("det") * dets, dets, axis=1)
    sizes = (half, fd, ft, tiles)
    shape = part_shape(fd, ft, tiles)
    tall = (left_weight.shape[0], right_weight.shape[0])
    weights = (left_weight.T, right_weight.T)
    if dets % LANES == 0:
        inputs = (time_stream, low, high, filter_taps.T, rows, tile_owner.reshape(1, -1), precision) + weights
        scratch = [VMEM(shape, BF16)] + partial_scratch(half, fd, ft, tiles, time_stream, precision)
        sky = call(functools.partial(whole_kernel, n_tm, n_det, sizes), inputs, scratch + gather_scratch(count, shape), tall, "whole")
    else:
        part = plain_partial_sums(time_stream, low, high, filter_taps, rows, tile_owner, precision, *sizes)
        sky = call(functools.partial(gather_kernel, n_tm, n_det), (part,) + weights, gather_scratch(count, shape), tall, "gather")
    return sky.reshape(TILE_DEV, -1)


def solution(mesh):
    return jax.shard_map(
        functools.partial(local, mesh.shape["tm"], mesh.shape["det"]),
        mesh=mesh,
        in_specs=(
            P("det", "tm"),
            P("det", None),
            P(),
            P(),
            P(),
            P(("tm", "det"), None),
            P(),
            P(("tm", "det")),
        ),
        out_specs=P(("tm", "det"), None),
        check_vma=False,
    )
```

time: 66.3 us -> 46.7 us (0.70)
  Pallas kernels: 56.6 us -> 43.3 us
  other arithmetic: 3.64 us -> 0 us
  local copies, waits for them, and re-layouts: 4.76 us -> 2.43 us
    pallas_call x3 -> x2, Pallas kernels: 56.6 us -> 43.3 us  [the longest x1 34.2 us: call(): pl.pallas_call(kernel, out_shape=jax.ShapeDtypeStruct((TILE_DEV,) + tall,...]
    reduce_sum x2 -> x0, other arithmetic: 1.7 us -> none  [the longest x1 0.91 us: owner_rows(): slot_rank = jnp.sum((same_owner & earlier).astype(jnp.int32), axis=1)]
    slice x1 -> x0, local copies, waits for them, and re-layouts: 1.4 us -> none  [local(): time_stream[:, -width:]]
    unnamed x4 -> x3, local copies, waits for them, and re-layouts: 2.52 us -> 1.67 us
    add x1 -> x0, other arithmetic: 0.67 us -> none  [owner_rows(): return tile_owner * TILE_DEV + slot_rank]
    pad x1 -> x0, other arithmetic: 0.67 us -> none  [partial_sums(): jnp.pad(taps.astype(F32), ((0, 0), (0, 2 * width - taps.shape[1])))]
where the time goes in v2:
time: 46.7 us; the launch traced here: 46.5 us
  Pallas kernels  43.3 us (93%)
  local copies, waits for them, and re-layouts  2.43 us (5%)
  between operations  0.83 us (2%)
    pallas_call x1, Pallas kernels, call(): pl.pallas_call(kernel, out_shape=jax.ShapeDtypeStruct((TILE_DEV,) + tall,...  34.2 us
    pallas_call x1, Pallas kernels, exchange_edges(): pl.pallas_call(functools.partial(edge_kernel, n_tm, n_det, width), out_sh...  9.11 us
    unnamed x3, local copies, waits for them, and re-layouts  1.67 us

profile of v2, /device:TPU:0, one launch (start us, length us, event | category | flops | bytes accessed | tf_op | source)
XLA Modules:
  0.0 46.5 jit_solution(2297487613883696409)
XLA Ops:
  0.0 0.0 copy-start
  0.8 9.1 %edges.1 = (bf16[128,128]{1,0:T(8,128)(2,1)}, bf16[128,128]{1,0:T(8,128)(2,1)}, s32[8,8,128]{2,1,0:T(8,128)}) custom-call(bf16[128,8192]{1,0:T(8,128)(2,1)} %refs_0_.1, s32[8,128]{1,0:T(8,128)} %bitcast.13, s32[1]{0:T(128)S(6)} %copy.12.count_ref), custom_call_target="tpu_custom_call" | custom-call | tf_op jit(solution)/shard_map/edges/pallas_call | solution.py:96
  9.9 0.0 copy-done
  9.9 0.8 %constant_dynamic-slice_fusion.refs_6_ = bf16[1024,128]{1,0:T(8,128)(2,1)} fusion(bf16[1024,1024]{1,0:T(8,128)(2,1)S(1)} %copy-done, s32[]{:T(128)S(6)} %select_n.3), kind=kLoop, calls=%fused_computation.1 | loop fusion | bytes 524292 | tf_op jit(solution)/shard_map/dynamic_slice | solution.py:361
  10.7 34.2 %whole.1 = f32[2,128,128]{2,1,0:T(8,128)} custom-call(bf16[128,8192]{1,0:T(8,128)(2,1)} %refs_0_.1, bf16[128,128]{1,0:T(8,128)(2,1)} %get-tuple-element.8.refs_1_, bf16[128,128]{1,0:T(8,128)(2,1)} %get-tuple-element.9.refs_2_, bf16[129,128]{1,0:T(8,128)(2,1)} %bitcast.10, s32[8,8,128]{2,1,0:T(8,128)} %get-tuple-element.10.refs_4_, s32[1,64]{1,0:T(1,128)} %bitcast.14, ...), custom_call_target="tpu_custom_call" | custom-call | tf_op jit(solution)/shard_map/whole/pallas_call | solution.py:339
  44.9 1.7 %copy.11 = f32[1,2,128,128]{3,1,2,0:T(2,128)} copy(f32[1,2,128,128]{3,2,1,0:T(8,128)} %bitcast.9) | data formatting | bytes 262144
Async XLA Ops:
  0.0 9.9 %copy-start = (bf16[1024,1024]{1,0:T(8,128)(2,1)S(1)}, bf16[1024,1024]{1,0:T(8,128)(2,1)}, u32[]{:S(2)}) copy-start(bf16[1024,1024]{1,0:T(8,128)(2,1)} %param.10) | copy-start | bytes 6291460

commit v3 on v2

--- a/solution.py
+++ b/solution.py
@@ -23,25 +23,9 @@
     return tile_owner * TILE_DEV + slot_rank
 
 
-def edge_kernel(n_tm, n_det, width, x_ref, tile_ref, count_ref, low_ref, high_ref, all_ref, rows_ref, send_sem, recv_sem, halo_send, halo_recv, own_sem):
+def start_edges(n_tm, n_det, width, x_ref, low_ref, high_ref, all_ref, rows_ref, send_sem, recv_sem, halo_send, halo_recv, own_sem):
     tm, det = lax.axis_index("tm"), lax.axis_index("det")
     has_low, has_high = tm > 0, tm < n_tm - 1
-    barrier = pltpu.get_barrier_semaphore()
-    for step in range(1, n_det):
-        pl.semaphore_signal(barrier, inc=1, device_id=(tm, lax.rem(det + step, n_det)), device_id_type=MESH)
-
-    @pl.when(has_low)
-    def _():
-        pl.semaphore_signal(barrier, inc=1, device_id=(tm - 1, det), device_id_type=MESH)
-
-    @pl.when(has_high)
-    def _():
-        pl.semaphore_signal(barrier, inc=1, device_id=(tm + 1, det), device_id_type=MESH)
-
-    tile = tile_ref[...]
-    frame = lax.broadcasted_iota(jnp.int32, tile.shape, 0) * tile.shape[1] + lax.broadcasted_iota(jnp.int32, tile.shape, 1)
-    rows_ref[...] = jnp.where(frame < count_ref[0], tile, -1)
-    pl.semaphore_wait(barrier, n_det - 1 + has_low.astype(jnp.int32) + has_high.astype(jnp.int32))
     down = pltpu.make_async_remote_copy(
         src_ref=x_ref.at[:, 0:width], dst_ref=high_ref, send_sem=halo_send.at[0], recv_sem=halo_recv.at[0],
         device_id=(tm - 1, det), device_id_type=MESH)
@@ -75,19 +59,58 @@
     def _():
         high_ref[...] = jnp.zeros_like(high_ref)
 
-    own.wait()
-    for copy in copies:
-        copy.wait()
+    def finish():
+        own.wait()
+        for copy in copies:
+            copy.wait()
+
+        @pl.when(has_low)
+        def _():
+            down.wait_send()
+            up.wait_recv()
+
+        @pl.when(has_high)
+        def _():
+            up.wait_send()
+            down.wait_recv()
+
+    return finish
+
+
+def live_rows(tile_ref, count_ref, rows_ref):
+    tile = tile_ref[...]
+    frame = lax.broadcasted_iota(jnp.int32, tile.shape, 0) * tile.shape[1] + lax.broadcasted_iota(jnp.int32, tile.shape, 1)
+    rows_ref[...] = jnp.where(frame < count_ref[0], tile, -1)
+
+
+def edge_kernel(n_tm, n_det, width, x_ref, tile_ref, count_ref, low_ref, high_ref, all_ref, rows_ref, *sems):
+    tm, det = lax.axis_index("tm"), lax.axis_index("det")
+    has_low, has_high = tm > 0, tm < n_tm - 1
+    barrier = pltpu.get_barrier_semaphore()
+    for step in range(1, n_det):
+        pl.semaphore_signal(barrier, inc=1, device_id=(tm, lax.rem(det + step, n_det)), device_id_type=MESH)
 
     @pl.when(has_low)
     def _():
-        down.wait_send()
-        up.wait_recv()
+        pl.semaphore_signal(barrier, inc=1, device_id=(tm - 1, det), device_id_type=MESH)
 
     @pl.when(has_high)
     def _():
-        up.wait_send()
-        down.wait_recv()
+        pl.semaphore_signal(barrier, inc=1, device_id=(tm + 1, det), device_id_type=MESH)
+
+    live_rows(tile_ref, count_ref, rows_ref)
+    pl.semaphore_wait(barrier, n_det - 1 + has_low.astype(jnp.int32) + has_high.astype(jnp.int32))
+    start_edges(n_tm, n_det, width, x_ref, low_ref, high_ref, all_ref, rows_ref, *sems)()
+
+
+def edge_sems(n_det):
+    return [
+        pltpu.SemaphoreType.DMA((n_det,)),
+        pltpu.SemaphoreType.DMA((n_det,)),
+        pltpu.SemaphoreType.DMA((2,)),
+        pltpu.SemaphoreType.DMA((2,)),
+        pltpu.SemaphoreType.DMA,
+    ]
 
 
 def exchange_edges(n_tm, n_det, width, x, tile, count):
@@ -100,12 +123,7 @@
         out_specs=(vmem,) * 3,
         scratch_shapes=[
             VMEM(tile.shape, tile.dtype),
-            pltpu.SemaphoreType.DMA((n_det,)),
-            pltpu.SemaphoreType.DMA((n_det,)),
-            pltpu.SemaphoreType.DMA((2,)),
-            pltpu.SemaphoreType.DMA((2,)),
-            pltpu.SemaphoreType.DMA,
-        ],
+        ] + edge_sems(n_det),
         compiler_params=pltpu.CompilerParams(collective_id=0, has_side_effects=True),
         name="edges",
     )(x, tile, count)
@@ -116,23 +134,24 @@
 
 
 def partial_body(
-    half, fd, ft, tiles,
-    x_ref, low_ref, high_ref, tapst_ref, rows_ref, owner_ref, prec_ref, out_ref,
-    wide, taps_ref, blocks, result, turned, picks, prec, cells, packed,
+    half, fd, ft, tiles, exchange,
+    x_hbm, tapst_ref, owner_ref, prec_hbm, low_ref, high_ref, rows_ref, out_ref,
+    x_ref, prec_ref, load_sem, wide, taps_ref, blocks, result, turned, picks, prec, cells, packed,
 ):
     dets, samples = x_ref.shape
+    first = pl.multiple_of(lax.axis_index("det") * dets, dets)
+    loads = [
+        pltpu.make_async_copy(x_hbm, x_ref, load_sem.at[0]),
+        pltpu.make_async_copy(prec_hbm.at[:, pl.ds(first, dets)], prec_ref, load_sem.at[1]),
+    ]
+    for load in loads:
+        load.start()
     width = 2 * half
     nblk = samples // width
     padded = blocks.shape[0] // dets - 1
     groups = prec_ref.shape[0] // fd
     columns = samples // ft
     contract = (((1,), (1,)), ((), ()))
-
-    blocks[0:dets, :] = low_ref[...].astype(F32)
-    for b in range(nblk):
-        blocks[(b + 1) * dets:(b + 2) * dets, :] = x_ref[:, b * width:(b + 1) * width].astype(F32)
-    blocks[(nblk + 1) * dets:(nblk + 2) * dets, :] = high_ref[...].astype(F32)
-    blocks[(nblk + 2) * dets:, :] = jnp.zeros((blocks.shape[0] - (nblk + 2) * dets, width), F32)
 
     wide[...] = jnp.zeros(wide.shape, F32)
     wide[0:tapst_ref.shape[0], :] = tapst_ref[...].astype(F32)
@@ -146,6 +165,17 @@
     place = across_owner * TILE_DEV + rank
     order = jnp.sum(jnp.where(place == down.astype(F32), across_tile.astype(F32), 0.0), axis=1, keepdims=True)
     order = jnp.broadcast_to(order, (tiles, columns))
+    loads[0].wait()
+    for b in range(nblk):
+        blocks[(b + 1) * dets:(b + 2) * dets, :] = x_ref[:, b * width:(b + 1) * width].astype(F32)
+    blocks[(nblk + 2) * dets:, :] = jnp.zeros((blocks.shape[0] - (nblk + 2) * dets, width), F32)
+    finish = exchange()
+    loads[1].wait()
+    for g in range(groups):
+        prec[:, g * dets:(g + 1) * dets] = prec_ref[g * fd:(g + 1) * fd, :]
+    finish()
+    blocks[0:dets, :] = low_ref[...].astype(F32)
+    blocks[(nblk + 1) * dets:(nblk + 2) * dets, :] = high_ref[...].astype(F32)
     per_row = rows_ref.shape[2] // (columns // rows_ref.shape[0])
     span = rows_ref.shape[2] // per_row
     for q in range(per_row):
@@ -153,8 +183,6 @@
         for r in range(rows.shape[0]):
             g = r * per_row + q
             picks[g * tiles:(g + 1) * tiles, :] = jnp.where(order == rows[r:r + 1, :], 1.0, 0.0).astype(BF16)
-    for g in range(groups):
-        prec[:, g * dets:(g + 1) * dets] = prec_ref[g * fd:(g + 1) * fd, :]
 
     unroll = divisor(dets, 16)
 
@@ -232,6 +260,9 @@
     groups = precision.shape[0] // fd
     across = LANES // fd
     return [
+        VMEM(x.shape, BF16),
+        VMEM((precision.shape[0], dets), BF16),
+        pltpu.SemaphoreType.DMA((2,)),
         VMEM((2 * width, dets), F32),
         VMEM((dets, 2 * width), F32),
         VMEM(((padded + 1) * dets, width), F32),
@@ -284,12 +315,12 @@
     return me, barrier
 
 
-def gather_body(n_tm, n_det, me, barrier, part_ref, left_ref, right_ref, out_ref, held, send_sem, recv_sem, own_sem):
+def gather_body(n_tm, n_det, me, part_ref, left_ref, right_ref, out_ref, held, send_sem, recv_sem, own_sem):
     count = n_tm * n_det
     fd = left_ref.shape[0]
-    pl.semaphore_wait(barrier, count - 1)
     copies = []
-    for step in range(1, count):
+    far = range(n_det, count)
+    for step in [*far, *range(1, n_det)]:
         other, where = peer(me, step, n_tm, n_det)
         copy = pltpu.make_async_remote_copy(
             src_ref=part_ref.at[other], dst_ref=held.at[me], send_sem=send_sem.at[step], recv_sem=recv_sem.at[step],
@@ -304,25 +335,36 @@
     total = jnp.sum(held[...].astype(F32), axis=0)
     low = total.shape[0] // TILE_DEV
     across = total.shape[1] // fd
+    tiles = []
     for k in range(TILE_DEV):
         tile = total[k * low:(k + 1) * low, :]
         stacked = jnp.concatenate([tile[:, v * fd:(v + 1) * fd] for v in range(across)], axis=0)
         rows = jnp.dot(stacked, left_ref[...], precision=lax.Precision.HIGHEST, preferred_element_type=F32)
-        out_ref[k] = lax.dot_general(
+        tiles.append(lax.dot_general(
             rows, right_ref[...], (((0,), (0,)), ((), ())), precision=lax.Precision.HIGHEST,
-            preferred_element_type=F32)
+            preferred_element_type=F32))
+    width = right_ref.shape[1]
+    for i in range(left_ref.shape[1]):
+        out_ref[:, i * width:(i + 1) * width] = jnp.concatenate([tile[i:i + 1, :] for tile in tiles], axis=0)
 
 
 def gather_kernel(n_tm, n_det, part_ref, left_ref, right_ref, out_ref, *scratch):
     me, barrier = greet(n_tm, n_det)
-    gather_body(n_tm, n_det, me, barrier, part_ref, left_ref, right_ref, out_ref, *scratch)
-
-
-def whole_kernel(n_tm, n_det, sizes, *refs):
-    ins, (left_ref, right_ref, out_ref, part), rest = refs[:7], refs[7:11], refs[11:]
+    pl.semaphore_wait(barrier, n_tm * n_det - 1)
+    gather_body(n_tm, n_det, me, part_ref, left_ref, right_ref, out_ref, *scratch)
+
+
+def whole_kernel(n_tm, n_det, sizes, x_ref, taps_ref, owner_ref, prec_ref, tile_ref, left_ref, right_ref, count_ref, out_ref, part, low, high, held_rows, own_rows, *rest):
+    edge, gather, scratch = rest[:5], rest[5:9], rest[9:]
+    live_rows(tile_ref, count_ref, own_rows)
     me, barrier = greet(n_tm, n_det)
-    partial_body(*sizes, *ins, part, *rest[:-4])
-    gather_body(n_tm, n_det, me, barrier, part, left_ref, right_ref, out_ref, *rest[-4:])
+
+    def exchange():
+        pl.semaphore_wait(barrier, n_tm * n_det - 1)
+        return start_edges(n_tm, n_det, 2 * sizes[0], x_ref, low, high, held_rows, own_rows, *edge)
+
+    partial_body(*sizes, exchange, x_ref, taps_ref, owner_ref, prec_ref, low, high, held_rows, part, *scratch)
+    gather_body(n_tm, n_det, me, part, left_ref, right_ref, out_ref, *gather)
 
 
 def gather_scratch(count, shape):
@@ -334,13 +376,12 @@
     ]
 
 
-def call(kernel, inputs, scratch, tall, name):
-    vmem = pl.BlockSpec(memory_space=VMEM)
+def call(kernel, specs, inputs, scratch, flat, name):
     return pl.pallas_call(
         kernel,
-        out_shape=jax.ShapeDtypeStruct((TILE_DEV,) + tall, F32),
-        in_specs=[vmem] * len(inputs),
-        out_specs=vmem,
+        out_shape=jax.ShapeDtypeStruct((TILE_DEV, flat), F32),
+        in_specs=[pl.BlockSpec(memory_space=space) for space in specs],
+        out_specs=pl.BlockSpec(memory_space=VMEM),
         scratch_shapes=scratch,
         compiler_params=pltpu.CompilerParams(
             collective_id=1, has_side_effects=True, vmem_limit_bytes=60 * 1024 * 1024),
@@ -357,20 +398,23 @@
     dets = time_stream.shape[0]
     tiles = tile_owner.shape[0]
     count = n_tm * n_det
-    low, high, rows = exchange_edges(n_tm, n_det, 2 * half, time_stream, frame_tile.reshape(-1, LANES), frame_count)
-    precision = lax.dynamic_slice_in_dim(det_precision, lax.axis_index("det") * dets, dets, axis=1)
+    tile = frame_tile.reshape(-1, LANES)
     sizes = (half, fd, ft, tiles)
     shape = part_shape(fd, ft, tiles)
-    tall = (left_weight.shape[0], right_weight.shape[0])
+    flat = left_weight.shape[0] * right_weight.shape[0]
     weights = (left_weight.T, right_weight.T)
+    gather = gather_scratch(count, shape)
     if dets % LANES == 0:
-        inputs = (time_stream, low, high, filter_taps.T, rows, tile_owner.reshape(1, -1), precision) + weights
-        scratch = [VMEM(shape, BF16)] + partial_scratch(half, fd, ft, tiles, time_stream, precision)
-        sky = call(functools.partial(whole_kernel, n_tm, n_det, sizes), inputs, scratch + gather_scratch(count, shape), tall, "whole")
-    else:
-        part = plain_partial_sums(time_stream, low, high, filter_taps, rows, tile_owner, precision, *sizes)
-        sky = call(functools.partial(gather_kernel, n_tm, n_det), (part,) + weights, gather_scratch(count, shape), tall, "gather")
-    return sky.reshape(TILE_DEV, -1)
+        inputs = (time_stream, filter_taps.T, tile_owner.reshape(1, -1), det_precision, tile) + weights + (frame_count,)
+        specs = (pl.ANY, VMEM, VMEM, pl.ANY, VMEM, VMEM, VMEM, pltpu.SMEM)
+        halo = VMEM((dets, 2 * half), BF16)
+        scratch = [VMEM(shape, BF16), halo, halo, VMEM((n_det,) + tile.shape, tile.dtype), VMEM(tile.shape, tile.dtype)]
+        scratch += edge_sems(n_det) + gather + partial_scratch(half, fd, ft, tiles, time_stream, det_precision)
+        return call(functools.partial(whole_kernel, n_tm, n_det, sizes), specs, inputs, scratch, flat, "whole")
+    low, high, rows = exchange_edges(n_tm, n_det, 2 * half, time_stream, tile, frame_count)
+    precision = lax.dynamic_slice_in_dim(det_precision, lax.axis_index("det") * dets, dets, axis=1)
+    part = plain_partial_sums(time_stream, low, high, filter_taps, rows, tile_owner, precision, *sizes)
+    return call(functools.partial(gather_kernel, n_tm, n_det), (VMEM,) * 3, (part,) + weights, gather, flat, "gather")
 
 
 def solution(mesh):

time: 46.7 us -> 44.1 us (0.944)
  Pallas kernels: 43.3 us -> 41.6 us
  local copies, waits for them, and re-layouts: 2.43 us -> 1.57 us
    pallas_call x2 -> x1, Pallas kernels: 43.3 us -> 41.6 us  [call(): pl.pallas_call(kernel, out_shape=jax.ShapeDtypeStruct((TILE_DEV, flat), F...]
    dynamic_slice x1 -> x0, local copies, waits for them, and re-layouts: 0.77 us -> none  [local(): lax.dynamic_slice_in_dim(det_precision, lax.axis_index('det') * dets, det...]
    unnamed x3 -> x1, local copies, waits for them, and re-layouts: 1.67 us -> 1.57 us
where the time goes in v3:
time: 44.1 us; the launch traced here: 43.9 us
  Pallas kernels  41.6 us (94%)
  local copies, waits for them, and re-layouts  1.57 us (4%)
  between operations  0.66 us (1%)
    pallas_call x1, Pallas kernels, call(): pl.pallas_call(kernel, out_shape=jax.ShapeDtypeStruct((TILE_DEV, flat), F...  41.6 us
    unnamed x1, local copies, waits for them, and re-layouts  1.57 us

profile of v3, /device:TPU:0, one launch (start us, length us, event | category | flops | bytes accessed | tf_op | source)
XLA Modules:
  0.0 43.9 jit_solution(14213978067379352540)
XLA Ops:
  0.7 41.6 %whole.1 = f32[2,16384]{1,0:T(2,128)} custom-call(bf16[128,8192]{1,0:T(8,128)(2,1)} %x_ref.1, bf16[129,128]{1,0:T(8,128)(2,1)} %bitcast.5, s32[1,64]{1,0:T(1,128)} %bitcast.9, bf16[1024,1024]{1,0:T(8,128)(2,1)} %prec_ref.1, s32[8,128]{1,0:T(8,128)} %bitcast.8, f32[32,128]{1,0:T(8,128)} %bitcast.6, f32[32,128]{1,0:T(8,128)} %bitcast.7, s32[1]{0:T(128)S(6)} %copy.10.count_ref), custom_call_target="tpu_custom_call" | custom-call | tf_op jit(solution)/shard_map/whole/pallas_call | solution.py:380
  42.3 1.6 %copy.11 = f32[2,16384]{1,0:T(2,128)} copy(f32[2,16384]{1,0:T(2,128)} %whole.1) | data formatting | bytes 262144
